TPU v7x, 512 devices: a whole 4x8x8 slice. The times are simulated.
512 devices in a mesh: ctx: 64 (over x, y_lo, z), fsdp: 8 (over y_hi, core).
Axes of the slice: x: 4, y: 8 (y_hi: 4, y_lo: 2; y = y_hi * 2 + y_lo), z: 8, core: 2. Of those that a mesh axis runs over, the one named last changes fastest.
Arguments:
- queries: bfloat16 [2, 16384, 2048], P(None, 'ctx', 'fsdp'), may hold values from -5.5 to 5.5
- keys_values: bfloat16 [2, 2, 16384, 2048], P(None, None, 'ctx', 'fsdp'), may hold values from -5.5 to 5.5
- block_mask: int32 [256, 32], P('ctx'), may hold values 0 or 1
- out_weight: bfloat16 [2048, 4096], P('fsdp'), may hold values from -3 to 3
Outputs:
- mixed: bfloat16 [2, 16384, 4096], P(None, 'ctx', 'fsdp')
All inputs are finite; a program needn't handle non-finite values. No bound on the sum of `block_mask` on one device may be relied on, other than what follows from the above.
Results may differ from a plain program's by a relative error of at most 0.0058.
Values may be sent and summed in bfloat16 or wider, within the bound.
A program may use at most 64 MiB of HBM per device.

v0:
```python
import math
import jax
import jax.numpy as jnp
from jax import lax
from jax.sharding import PartitionSpec as P

HD = 128
BLK = 64
WINB = 32


def passed_along(array, axis, by):
    devices = lax.axis_size(axis)
    pairs = [(i, i + by) for i in range(devices) if 0 <= i + by < devices]
    return lax.ppermute(array, axis, pairs)


def block_rules(first_block, query_count, key_start, key_count, mask_rows):
    query_blocks = first_block + jnp.arange(query_count, dtype=jnp.int32)
    key_blocks = key_start + jnp.arange(key_count, dtype=jnp.int32)
    block_gap = query_blocks[:, None] - key_blocks[None, :]
    present = key_blocks[None, :] >= 0
    clean_ok = (block_gap >= 0) & (block_gap < WINB) & present
    offsets = jnp.arange(WINB, dtype=jnp.int32)
    picked = ((block_gap - 1)[:, :, None] == offsets[None, None, :]) & (mask_rows[:, None, :] == 1)
    noisy_ok = jnp.any(picked, axis=2) & present
    own_block = query_blocks[:, None] == query_blocks[None, :]

    def widen(table):
        return jnp.repeat(jnp.repeat(table, BLK, axis=0), BLK, axis=1)

    return (widen(clean_ok), widen(noisy_ok), widen(own_block))


def attend(query, keys, values, allowed):
    count, width = query.shape
    heads = width // HD
    query_three = query.reshape(count, heads, HD)
    key_three = keys.reshape(-1, heads, HD)
    value_three = values.reshape(-1, heads, HD)
    scores = jnp.einsum(
        "qhd,khd->hqk", query_three, key_three, preferred_element_type=jnp.float32
    ) * (1.0 / math.sqrt(HD))
    scores = jnp.where(allowed[None], scores, jnp.float32(-1e30))
    top = jnp.max(scores, axis=-1, keepdims=True)
    expo = jnp.exp(scores - top)
    weights = (expo / jnp.sum(expo, axis=-1, keepdims=True)).astype(jnp.bfloat16)
    result = jnp.einsum("hqk,khd->qhd", weights, value_three, preferred_element_type=jnp.float32)
    return result.reshape(count, width).astype(jnp.bfloat16)


def on_device(queries, keys_values, block_mask, out_weight):
    tokens = queries.shape[1]
    blocks_here = tokens // BLK
    reach = WINB * BLK // tokens
    own = keys_values[:, 0]
    pieces = []
    moving = own
    for step in range(reach):
        moving = passed_along(moving, "ctx", 1)
        pieces.insert(0, moving)
    window = jnp.concatenate(pieces + [own], axis=1)
    first_block = lax.axis_index("ctx") * blocks_here
    clean_ok, noisy_ok, own_ok = block_rules(
        first_block, blocks_here, first_block - WINB, blocks_here + WINB, block_mask
    )
    clean_out = attend(queries[0], window[0], window[1], clean_ok)
    noisy_keys = jnp.concatenate([window[0], keys_values[0, 1]], axis=0)
    noisy_values = jnp.concatenate([window[1], keys_values[1, 1]], axis=0)
    noisy_allowed = jnp.concatenate([noisy_ok, own_ok], axis=1)
    noisy_out = attend(queries[1], noisy_keys, noisy_values, noisy_allowed)
    attended = jnp.stack([clean_out, noisy_out])
    panel = lax.all_to_all(out_weight, "fsdp", split_axis=1, concat_axis=0, tiled=True)
    piece = lax.all_gather(attended, "fsdp", axis=2, tiled=True)
    columns = piece.shape[2]
    mixed = jnp.dot(piece.reshape(-1, columns), panel, preferred_element_type=jnp.float32)
    return mixed.astype(jnp.bfloat16).reshape(2, tokens, panel.shape[1])


def solution(mesh):
    in_specs = (
        P(None, "ctx", "fsdp"),
        P(None, None, "ctx", "fsdp"),
        P("ctx", None),
        P("fsdp", None),
    )
    out_specs = P(None, "ctx", "fsdp")
    return jax.shard_map(
        on_device, mesh=mesh, in_specs=in_specs, out_specs=out_specs, check_vma=False
    )
```

profile of v0, /device:TPU:1, one launch (start us, length us, event | category | flops | bytes accessed | tf_op | source)
XLA Modules:
  0.0 229.4 jit_solution(5361212706410624374)
XLA Ops:
  6.5 1.0 slice.23
  7.6 4.8 %collective-permute-start = (bf16[2,256,256]{1,2,0:T(8,128)(2,1)S(1)}, bf16[2,256,256]{1,2,0:T(8,128)(2,1)S(1)}, u32[]{:S(2)}, u32[]{:S(2)}) collective-permute-start(bf16[2,256,256]{1,2,0:T(8,128)(2,1)S(1)} %bitcast.72), channel_id=1, source_target_pairs={{0,8},{8,16},{16,24},{24,32},{32,40},{40,48},{48,56},{56,64},{64,7... | collective-permute-start | bytes 786440 | tf_op jit(solution)/shard_map/ppermute | solution.py:15
  12.5 3.3 %collective-permute-done = bf16[2,256,256]{1,2,0:T(8,128)(2,1)S(1)} collective-permute-done((bf16[2,256,256]{1,2,0:T(8,128)(2,1)S(1)}, bf16[2,256,256]{1,2,0:T(8,128)(2,1)S(1)}, u32[]{:S(2)}, u32[]{:S(2)}) %collective-permute-start) | collective-permute-done | bytes 262176 | tf_op jit(solution)/shard_map/ppermute | solution.py:15
  15.8 5.7 %collective-permute-start.1 = (bf16[2,256,256]{1,2,0:T(8,128)(2,1)S(1)}, bf16[2,256,256]{1,2,0:T(8,128)(2,1)S(1)}, u32[]{:S(2)}, u32[]{:S(2)}) collective-permute-start(bf16[2,256,256]{1,2,0:T(8,128)(2,1)S(1)} %collective-permute-done), channel_id=1, source_target_pairs={{0,8},{8,16},{16,24},{24,32},{32,40},{40,48},{48,56},{56,64},{64,7... | collective-permute-start | bytes 786440 | tf_op jit(solution)/shard_map/ppermute | solution.py:15
  21.4 3.3 %collective-permute-done.1 = bf16[2,256,256]{1,2,0:T(8,128)(2,1)S(1)} collective-permute-done((bf16[2,256,256]{1,2,0:T(8,128)(2,1)S(1)}, bf16[2,256,256]{1,2,0:T(8,128)(2,1)S(1)}, u32[]{:S(2)}, u32[]{:S(2)}) %collective-permute-start.1) | collective-permute-done | bytes 262176 | tf_op jit(solution)/shard_map/ppermute | solution.py:15
  24.7 5.5 %collective-permute-start.2 = (bf16[2,256,256]{1,2,0:T(8,128)(2,1)S(1)}, bf16[2,256,256]{1,2,0:T(8,128)(2,1)}, u32[]{:S(2)}, u32[]{:S(2)}) collective-permute-start(bf16[2,256,256]{1,2,0:T(8,128)(2,1)S(1)} %collective-permute-done.1), channel_id=1, source_target_pairs={{0,8},{8,16},{16,24},{24,32},{32,40},{40,48},{48,56},{56,64},{64,7... | collective-permute-start | bytes 786440 | tf_op jit(solution)/shard_map/ppermute | solution.py:15
  30.3 4.1 %copy.58 = bf16[256,4096]{0,1:T(8,128)(2,1)} copy(bf16[256,4096]{1,0:T(8,128)(2,1)} %param.7) | data formatting | bytes 4194304 | tf_op args[3]
  34.4 10.1 %all-to-all-start = ((bf16[256,8,512]{0,2,1:T(8,128)(2,1)}), bf16[256,8,512]{0,2,1:T(8,128)(2,1)S(1)}, u32[]{:S(2)}, u32[]{:S(2)}) async-start(bf16[256,8,512]{0,2,1:T(8,128)(2,1)} %bitcast.64), calls=%async_computation | async-start | bytes 4194304 | tf_op jit(solution)/shard_map/all_to_all | solution.py:73
  44.5 4.3 %collective-permute-start.3 = (bf16[2,256,256]{1,2,0:T(8,128)(2,1)}, bf16[2,256,256]{1,2,0:T(8,128)(2,1)S(1)}, u32[]{:S(2)}, u32[]{:S(2)}) collective-permute-start(bf16[2,256,256]{1,2,0:T(8,128)(2,1)} %collective-permute-done.2), channel_id=1, source_target_pairs={{0,8},{8,16},{16,24},{24,32},{32,40},{40,48},{48,56},{56,64},{64,7... | collective-permute-start | bytes 786440 | tf_op jit(solution)/shard_map/ppermute | solution.py:15
  48.9 5.9 %collective-permute-done.3 = bf16[2,256,256]{1,2,0:T(8,128)(2,1)S(1)} collective-permute-done((bf16[2,256,256]{1,2,0:T(8,128)(2,1)}, bf16[2,256,256]{1,2,0:T(8,128)(2,1)S(1)}, u32[]{:S(2)}, u32[]{:S(2)}) %collective-permute-start.3) | collective-permute-done | bytes 262176 | tf_op jit(solution)/shard_map/ppermute | solution.py:15
  54.8 5.3 %collective-permute-start.4 = (bf16[2,256,256]{1,2,0:T(8,128)(2,1)S(1)}, bf16[2,256,256]{1,2,0:T(8,128)(2,1)S(1)}, u32[]{:S(2)}, u32[]{:S(2)}) collective-permute-start(bf16[2,256,256]{1,2,0:T(8,128)(2,1)S(1)} %collective-permute-done.3), channel_id=1, source_target_pairs={{0,8},{8,16},{16,24},{24,32},{32,40},{40,48},{48,56},{56,64},{64,7... | collective-permute-start | bytes 786440 | tf_op jit(solution)/shard_map/ppermute | solution.py:15
  60.2 4.6 %collective-permute-done.4 = bf16[2,256,256]{1,2,0:T(8,128)(2,1)S(1)} collective-permute-done((bf16[2,256,256]{1,2,0:T(8,128)(2,1)S(1)}, bf16[2,256,256]{1,2,0:T(8,128)(2,1)S(1)}, u32[]{:S(2)}, u32[]{:S(2)}) %collective-permute-start.4) | collective-permute-done | bytes 262176 | tf_op jit(solution)/shard_map/ppermute | solution.py:15
  64.8 6.0 %collective-permute-start.5 = (bf16[2,256,256]{1,2,0:T(8,128)(2,1)S(1)}, bf16[2,256,256]{1,2,0:T(8,128)(2,1)}, u32[]{:S(2)}, u32[]{:S(2)}) collective-permute-start(bf16[2,256,256]{1,2,0:T(8,128)(2,1)S(1)} %collective-permute-done.4), channel_id=1, source_target_pairs={{0,8},{8,16},{16,24},{24,32},{32,40},{40,48},{48,56},{56,64},{64,7... | collective-permute-start | bytes 786440 | tf_op jit(solution)/shard_map/ppermute | solution.py:15
  71.0 3.0 %collective-permute-done.5 = bf16[2,256,256]{1,2,0:T(8,128)(2,1)} collective-permute-done((bf16[2,256,256]{1,2,0:T(8,128)(2,1)S(1)}, bf16[2,256,256]{1,2,0:T(8,128)(2,1)}, u32[]{:S(2)}, u32[]{:S(2)}) %collective-permute-start.5) | collective-permute-done | bytes 262176 | tf_op jit(solution)/shard_map/ppermute | solution.py:15
  74.0 4.2 %collective-permute-start.6 = (bf16[2,256,256]{1,2,0:T(8,128)(2,1)}, bf16[2,256,256]{1,2,0:T(8,128)(2,1)S(1)}, u32[]{:S(2)}, u32[]{:S(2)}) collective-permute-start(bf16[2,256,256]{1,2,0:T(8,128)(2,1)} %collective-permute-done.5), channel_id=1, source_target_pairs={{0,8},{8,16},{16,24},{24,32},{32,40},{40,48},{48,56},{56,64},{64,7... | collective-permute-start | bytes 786440 | tf_op jit(solution)/shard_map/ppermute | solution.py:15
  82.9 4.1 %collective-permute-start.7 = (bf16[2,256,256]{1,2,0:T(8,128)(2,1)S(1)}, bf16[2,256,256]{1,2,0:T(8,128)(2,1)S(1)}, u32[]{:S(2)}, u32[]{:S(2)}) collective-permute-start(bf16[2,256,256]{1,2,0:T(8,128)(2,1)S(1)} %collective-permute-done.6), channel_id=1, source_target_pairs={{0,8},{8,16},{16,24},{24,32},{32,40},{40,48},{48,56},{56,64},{64,7... | collective-permute-start | bytes 786440 | tf_op jit(solution)/shard_map/ppermute | solution.py:15
  87.9 1.1 pad_add_fusion
  89.0 1.3 collective-permute-done.7
  90.4 1.0 constant_dynamic-update-slice_fusion.6
  91.4 1.0 constant_dynamic-update-slice_fusion.3
  92.5 1.2 fusion.53
  93.6 1.4 copy.51
  95.0 1.0 broadcast_in_dim.58
  96.0 2.9 %fusion.58 = f32[2,256]{1,0:T(2,128)S(1)} fusion(bf16[2304,2,128]{0,2,1:T(8,128)(2,1)S(1)} %bitcast.66, bf16[256,2,128]{0,2,1:T(8,128)(2,1)S(1)} %bitcast.77, pred[256,2304]{0,1:T(8,128)(4,1)} %bitcast.73), kind=kOutput, calls=%fused_computation.66 | convolution fusion | flops 306710784 | bytes 1902592 | tf_op jit(solution)/shard_map/sub | solution.py:46
  98.9 4.4 %fusion.15 = bf16[2,128,256]{2,1,0:T(8,128)(2,1)} fusion(bf16[2304,2,128]{0,2,1:T(8,128)(2,1)} %bitcast.70, f32[2,256]{1,0:T(2,128)S(1)} %fusion.58, bf16[2304,2,128]{0,2,1:T(8,128)(2,1)S(1)} %bitcast.67, bf16[256,2,128]{0,2,1:T(8,128)(2,1)S(1)} %bitcast.78, pred[256,2304]{0,1:T(8,128)(4,1)} %bitcast.74), kind=kOutput, calls=%fused_computation.22 | convolution fusion | flops 609946368 | bytes 3213312 | tf_op jit(solution)/shard_map/hqk,khd->qhd/dot_general | solution.py:48
  103.3 1.0 copy.56
  104.4 3.4 %exponential_reduce_fusion = f32[2,256]{1,0:T(2,128)S(1)} fusion(bf16[256,2,128]{0,2,1:T(8,128)(2,1)} %bitcast.79, pred[256,2560]{0,1:T(8,128)(4,1)} %pad_add_fusion, bf16[256,2,128]{2,0,1:T(8,128)(2,1)S(1)} %copy-done.12, bf16[2304,2,128]{2,0,1:T(8,128)(2,1)} %copy.51), kind=kOutput, calls=%fused_computation.7 | convolution fusion | flops 343411200 | bytes 2099200 | tf_op jit(solution)/shard_map/sub | solution.py:46
  107.8 4.5 %fusion.16 = bf16[2,128,256]{2,1,0:T(8,128)(2,1)} fusion(f32[2,256]{1,0:T(2,128)S(1)} %exponential_reduce_fusion, bf16[256,2,128]{0,2,1:T(8,128)(2,1)} %bitcast.81, bf16[2304,2,128]{0,2,1:T(8,128)(2,1)} %bitcast.71, bf16[256,2,128]{0,2,1:T(8,128)(2,1)} %bitcast.80, pred[256,2560]{0,1:T(8,128)(4,1)} %pad_add_fusion, bf16[256,2,128]{2,0,1:T(8,128)(2,1)S(1)} %copy-done.12, ...), kind=kOutput, calls=%fused_computation.23 | convolution fusion | flops 682953728 | bytes 3540992 | tf_op jit(solution)/shard_map/hqk,khd->qhd/dot_general | solution.py:48
  112.3 1.0 copy.57
  114.1 2.4 %copy.59 = bf16[8,256,512]{2,1,0:T(8,128)(2,1)} copy(bf16[8,256,512]{1,2,0:T(8,128)(2,1)S(1)} %bitcast.63) | data formatting | bytes 4194304 | tf_op jit(solution)/shard_map/all_to_all | solution.py:73
  116.5 101.8 %all-gather.2.cloned.1.call-done = bf16[2,256,2048]{2,1,0:T(8,128)(2,1)} async-done(((bf16[2,256,256]{2,1,0:T(8,128)(2,1)}), bf16[2,256,2048]{2,1,0:T(8,128)(2,1)}) %all-gather.2.cloned.1.call-update) | async-done | bytes 2097168 | tf_op jit(solution)/shard_map/all_gather | solution.py:74
  218.3 4.3 %convolution_convert_fusion = bf16[512,512]{1,0:T(8,128)(2,1)} fusion(bf16[512,2048]{1,0:T(8,128)(2,1)} %bitcast.84, bf16[2048,512]{1,0:T(8,128)(2,1)} %bitcast.69), kind=kOutput, calls=%fused_computation.21 | convolution fusion | flops 1074003968 | bytes 4718592 | tf_op jit(solution)/shard_map/dot_general | solution.py:76
  (67 shorter events, 6.9 us)
Async XLA Ops:
  7.6 8.1 %collective-permute-start = (bf16[2,256,256]{1,2,0:T(8,128)(2,1)S(1)}, bf16[2,256,256]{1,2,0:T(8,128)(2,1)S(1)}, u32[]{:S(2)}, u32[]{:S(2)}) collective-permute-start(bf16[2,256,256]{1,2,0:T(8,128)(2,1)S(1)} %bitcast.72), channel_id=1, source_target_pairs={{0,8},{8,16},{16,24},{24,32},{32,40},{40,48},{48,56},{56,64},{64,7... | collective-permute-start | bytes 786440 | tf_op jit(solution)/shard_map/ppermute | solution.py:15
  15.8 18.6 %copy-start.3 = (bf16[2,256,256]{1,2,0:T(8,128)(2,1)}, bf16[2,256,256]{1,2,0:T(8,128)(2,1)S(1)}, u32[]{:S(2)}) copy-start(bf16[2,256,256]{1,2,0:T(8,128)(2,1)S(1)} %collective-permute-done) | copy-start | bytes 786436
  15.8 8.9 %collective-permute-start.1 = (bf16[2,256,256]{1,2,0:T(8,128)(2,1)S(1)}, bf16[2,256,256]{1,2,0:T(8,128)(2,1)S(1)}, u32[]{:S(2)}, u32[]{:S(2)}) collective-permute-start(bf16[2,256,256]{1,2,0:T(8,128)(2,1)S(1)} %collective-permute-done), channel_id=1, source_target_pairs={{0,8},{8,16},{16,24},{24,32},{32,40},{40,48},{48,56},{56,64},{64,7... | collective-permute-start | bytes 786440 | tf_op jit(solution)/shard_map/ppermute | solution.py:15
  24.7 9.6 %copy-start.5 = (bf16[2,256,256]{1,2,0:T(8,128)(2,1)}, bf16[2,256,256]{1,2,0:T(8,128)(2,1)S(1)}, u32[]{:S(2)}) copy-start(bf16[2,256,256]{1,2,0:T(8,128)(2,1)S(1)} %collective-permute-done.1) | copy-start | bytes 786436
  24.7 19.7 %collective-permute-start.2 = (bf16[2,256,256]{1,2,0:T(8,128)(2,1)S(1)}, bf16[2,256,256]{1,2,0:T(8,128)(2,1)}, u32[]{:S(2)}, u32[]{:S(2)}) collective-permute-start(bf16[2,256,256]{1,2,0:T(8,128)(2,1)S(1)} %collective-permute-done.1), channel_id=1, source_target_pairs={{0,8},{8,16},{16,24},{24,32},{32,40},{40,48},{48,56},{56,64},{64,7... | collective-permute-start | bytes 786440 | tf_op jit(solution)/shard_map/ppermute | solution.py:15
  34.3 25.8 %copy-start.13 = (s32[4,32]{1,0:T(4,128)S(1)}, s32[4,32]{1,0:T(4,128)}, u32[]{:S(2)}) copy-start(s32[4,32]{1,0:T(4,128)} %param.6) | copy-start | bytes 1540
  34.3 36.6 %copy-start.2 = (bf16[2,256,256]{2,1,0:T(8,128)(2,1)S(1)}, bf16[2,256,256]{2,1,0:T(8,128)(2,1)}, u32[]{:S(2)}) copy-start(bf16[2,256,256]{2,1,0:T(8,128)(2,1)} %param.4) | copy-start | bytes 786436
  34.3 46.1 %copy-start.1 = (bf16[2,2,256,256]{3,2,1,0:T(8,128)(2,1)S(1)}, bf16[2,2,256,256]{3,2,1,0:T(8,128)(2,1)}, u32[]{:S(2)}) copy-start(bf16[2,2,256,256]{3,2,1,0:T(8,128)(2,1)} %param.5) | copy-start | bytes 1572868
  34.4 79.7 %all-to-all-start = ((bf16[256,8,512]{0,2,1:T(8,128)(2,1)}), bf16[256,8,512]{0,2,1:T(8,128)(2,1)S(1)}, u32[]{:S(2)}, u32[]{:S(2)}) async-start(bf16[256,8,512]{0,2,1:T(8,128)(2,1)} %bitcast.64), calls=%async_computation | async-start | bytes 4194304 | tf_op jit(solution)/shard_map/all_to_all | solution.py:73
  44.5 173.8 %all-gather.2.cloned.1.call-start = ((), (), s32[]{:S(2)}) async-start(), calls=%async_computation.1 | async-start | bytes 2359296 | tf_op jit(solution)/shard_map/all_gather | solution.py:74
  44.5 10.3 %collective-permute-start.3 = (bf16[2,256,256]{1,2,0:T(8,128)(2,1)}, bf16[2,256,256]{1,2,0:T(8,128)(2,1)S(1)}, u32[]{:S(2)}, u32[]{:S(2)}) collective-permute-start(bf16[2,256,256]{1,2,0:T(8,128)(2,1)} %collective-permute-done.2), channel_id=1, source_target_pairs={{0,8},{8,16},{16,24},{24,32},{32,40},{40,48},{48,56},{56,64},{64,7... | collective-permute-start | bytes 786440 | tf_op jit(solution)/shard_map/ppermute | solution.py:15
  54.8 16.1 %copy-start.7 = (bf16[2,256,256]{1,2,0:T(8,128)(2,1)}, bf16[2,256,256]{1,2,0:T(8,128)(2,1)S(1)}, u32[]{:S(2)}) copy-start(bf16[2,256,256]{1,2,0:T(8,128)(2,1)S(1)} %collective-permute-done.3) | copy-start | bytes 786436
  54.8 10.1 %collective-permute-start.4 = (bf16[2,256,256]{1,2,0:T(8,128)(2,1)S(1)}, bf16[2,256,256]{1,2,0:T(8,128)(2,1)S(1)}, u32[]{:S(2)}, u32[]{:S(2)}) collective-permute-start(bf16[2,256,256]{1,2,0:T(8,128)(2,1)S(1)} %collective-permute-done.3), channel_id=1, source_target_pairs={{0,8},{8,16},{16,24},{24,32},{32,40},{40,48},{48,56},{56,64},{64,7... | collective-permute-start | bytes 786440 | tf_op jit(solution)/shard_map/ppermute | solution.py:15
  64.8 6.1 %copy-start.9 = (bf16[2,256,256]{1,2,0:T(8,128)(2,1)}, bf16[2,256,256]{1,2,0:T(8,128)(2,1)S(1)}, u32[]{:S(2)}) copy-start(bf16[2,256,256]{1,2,0:T(8,128)(2,1)S(1)} %collective-permute-done.4) | copy-start | bytes 786436
  64.8 9.2 %collective-permute-start.5 = (bf16[2,256,256]{1,2,0:T(8,128)(2,1)S(1)}, bf16[2,256,256]{1,2,0:T(8,128)(2,1)}, u32[]{:S(2)}, u32[]{:S(2)}) collective-permute-start(bf16[2,256,256]{1,2,0:T(8,128)(2,1)S(1)} %collective-permute-done.4), channel_id=1, source_target_pairs={{0,8},{8,16},{16,24},{24,32},{32,40},{40,48},{48,56},{56,64},{64,7... | collective-permute-start | bytes 786440 | tf_op jit(solution)/shard_map/ppermute | solution.py:15
  74.0 8.9 %collective-permute-start.6 = (bf16[2,256,256]{1,2,0:T(8,128)(2,1)}, bf16[2,256,256]{1,2,0:T(8,128)(2,1)S(1)}, u32[]{:S(2)}, u32[]{:S(2)}) collective-permute-start(bf16[2,256,256]{1,2,0:T(8,128)(2,1)} %collective-permute-done.5), channel_id=1, source_target_pairs={{0,8},{8,16},{16,24},{24,32},{32,40},{40,48},{48,56},{56,64},{64,7... | collective-permute-start | bytes 786440 | tf_op jit(solution)/shard_map/ppermute | solution.py:15
  80.5 10.8 %copy-start.10 = (bf16[2,256,256]{1,2,0:T(8,128)(2,1)S(1)}, bf16[2,256,256]{1,2,0:T(8,128)(2,1)}, u32[]{:S(2)}) copy-start(bf16[2,256,256]{1,2,0:T(8,128)(2,1)} %copy-done.9) | copy-start | bytes 786436
  81.4 10.0 %copy-start.8 = (bf16[2,256,256]{1,2,0:T(8,128)(2,1)S(1)}, bf16[2,256,256]{1,2,0:T(8,128)(2,1)}, u32[]{:S(2)}) copy-start(bf16[2,256,256]{1,2,0:T(8,128)(2,1)} %copy-done.7) | copy-start | bytes 786436
  82.9 7.4 %collective-permute-start.7 = (bf16[2,256,256]{1,2,0:T(8,128)(2,1)S(1)}, bf16[2,256,256]{1,2,0:T(8,128)(2,1)S(1)}, u32[]{:S(2)}, u32[]{:S(2)}) collective-permute-start(bf16[2,256,256]{1,2,0:T(8,128)(2,1)S(1)} %collective-permute-done.6), channel_id=1, source_target_pairs={{0,8},{8,16},{16,24},{24,32},{32,40},{40,48},{48,56},{56,64},{64,7... | collective-permute-start | bytes 786440 | tf_op jit(solution)/shard_map/ppermute | solution.py:15
  87.9 4.5 %copy-start.6 = (bf16[2,256,256]{1,2,0:T(8,128)(2,1)S(1)}, bf16[2,256,256]{1,2,0:T(8,128)(2,1)}, u32[]{:S(2)}) copy-start(bf16[2,256,256]{1,2,0:T(8,128)(2,1)} %copy-done.5) | copy-start | bytes 786436
  87.9 4.5 %copy-start.4 = (bf16[2,256,256]{1,2,0:T(8,128)(2,1)S(1)}, bf16[2,256,256]{1,2,0:T(8,128)(2,1)}, u32[]{:S(2)}) copy-start(bf16[2,256,256]{1,2,0:T(8,128)(2,1)} %copy-done.3) | copy-start | bytes 786436
  93.6 2.4 %copy-start.11 = (bf16[1,256,256]{1,2,0:T(8,128)(2,1)S(1)}, bf16[1,256,256]{1,2,0:T(8,128)(2,1)}, u32[]{:S(2)}) copy-start(bf16[1,256,256]{1,2,0:T(8,128)(2,1)} %copy.66) | copy-start | bytes 393220
  98.9 5.4 %copy-start.12 = (bf16[256,2,128]{2,0,1:T(8,128)(2,1)S(1)}, bf16[256,2,128]{2,0,1:T(8,128)(2,1)}, u32[]{:S(2)}) copy-start(bf16[256,2,128]{2,0,1:T(8,128)(2,1)} %copy.52) | copy-start | bytes 393220
  104.4 3.4 %copy-start = (bf16[2304,2,128]{2,0,1:T(8,128)(2,1)S(1)}, bf16[2304,2,128]{2,0,1:T(8,128)(2,1)}, u32[]{:S(2)}) copy-start(bf16[2304,2,128]{2,0,1:T(8,128)(2,1)} %copy.51) | copy-start | bytes 3538948
Sparse Core Ops, SparseCore 0:
  114.2 104.0 all-gather.1
where the time goes:
time: 230 us; the launch traced here: 229 us
  waiting for transfers between devices  123 us (53%)
  starting transfers between devices  50.1 us (22%)
  local copies, waits for them, and re-layouts  20.7 us (9%)
  matrix products  19.5 us (8%)
  between operations  13.7 us (6%)
    all_gather x1, waiting for transfers between devices, on_device(): piece = lax.all_gather(attended, 'fsdp', axis=2, tiled=True)  102 us
    ppermute x8, starting transfers between devices, passed_along(): return lax.ppermute(array, axis, pairs)  40 us
    ppermute x8, waiting for transfers between devices, passed_along(): return lax.ppermute(array, axis, pairs)  21.4 us
    all_to_all x1, starting transfers between devices, on_device(): lax.all_to_all(out_weight, 'fsdp', split_axis=1, concat_axis=0, tiled=True)  10.1 us
    dot_general x2, matrix products, attend(): jnp.einsum('hqk,khd->qhd', weights, value_three, preferred_element_type=j...  8.93 us
    unnamed x41, local copies, waits for them, and re-layouts  7.94 us
    sub x2, matrix products, attend(): expo = jnp.exp(scores - top)  6.32 us
  transfers between devices with their start and end apart: 10, of which 7 were waited for; matrix products, arithmetic and copies ran while one was open for 16% of the time, Pallas kernels for 0%

commit v1 on v0

--- a/solution.py
+++ b/solution.py
@@ -71,7 +71,9 @@
     noisy_out = attend(queries[1], noisy_keys, noisy_values, noisy_allowed)
     attended = jnp.stack([clean_out, noisy_out])
     panel = lax.all_to_all(out_weight, "fsdp", split_axis=1, concat_axis=0, tiled=True)
-    piece = lax.all_gather(attended, "fsdp", axis=2, tiled=True)
+    piece = jnp.concatenate(
+        lax.all_to_all(jnp.stack([attended] * lax.axis_size("fsdp")), "fsdp", 0, 0), axis=2
+    )
     columns = piece.shape[2]
     mixed = jnp.dot(piece.reshape(-1, columns), panel, preferred_element_type=jnp.float32)
     return mixed.astype(jnp.bfloat16).reshape(2, tokens, panel.shape[1])

time: 230 us -> 238 us (1.035)
  the two profiles are of different devices: /device:TPU:1 before, /device:TPU:6 now
where the time goes in v1:
time: 238 us; the launch traced here: 237 us
  waiting for transfers between devices  163 us (68%)
  starting transfers between devices  29.2 us (12%)
  local copies, waits for them, and re-layouts  24.6 us (10%)
  matrix products  17.6 us (7%)
    ppermute x8, waiting for transfers between devices, passed_along(): return lax.ppermute(array, axis, pairs)  113 us
    all_to_all x1, waiting for transfers between devices, on_device(): lax.all_to_all(jnp.stack([attended] * lax.axis_size('fsdp')), 'fsdp', 0, 0)  49.8 us
    ppermute x8, starting transfers between devices, passed_along(): return lax.ppermute(array, axis, pairs)  17.7 us
    unnamed x46, local copies, waits for them, and re-layouts  9.5 us
    dot_general x2, matrix products, attend(): jnp.einsum('hqk,khd->qhd', weights, value_three, preferred_element_type=j...  9.34 us
    all_to_all x1, starting transfers between devices, on_device(): lax.all_to_all(out_weight, 'fsdp', split_axis=1, concat_axis=0, tiled=True)  6.35 us
    sub x2, matrix products, attend(): expo = jnp.exp(scores - top)  6.18 us
    all_to_all x1, starting transfers between devices, on_device(): lax.all_to_all(jnp.stack([attended] * lax.axis_size('fsdp')), 'fsdp', 0, 0)  5.21 us
  transfers between devices with their start and end apart: 10, of which 8 were waited for; matrix products, arithmetic and copies ran while one was open for 15% of the time, Pallas kernels for 0%

profile of v1, /device:TPU:6, one launch (start us, length us, event | category | flops | bytes accessed | tf_op | source)
XLA Modules:
  0.0 237.3 jit_solution(4489093504674853448)
XLA Ops:
  1.1 4.3 %collective-permute-start = (bf16[2,256,256]{1,2,0:T(8,128)(2,1)S(1)}, bf16[2,256,256]{1,2,0:T(8,128)(2,1)S(1)}, u32[]{:S(2)}, u32[]{:S(2)}) collective-permute-start(bf16[2,256,256]{1,2,0:T(8,128)(2,1)S(1)} %bitcast.77), channel_id=1, source_target_pairs={{0,8},{8,16},{16,24},{24,32},{32,40},{40,48},{48,56},{56,64},{64,7... | collective-permute-start | bytes 786440 | tf_op jit(solution)/shard_map/ppermute | solution.py:15
  5.4 14.2 %collective-permute-done = bf16[2,256,256]{1,2,0:T(8,128)(2,1)S(1)} collective-permute-done((bf16[2,256,256]{1,2,0:T(8,128)(2,1)S(1)}, bf16[2,256,256]{1,2,0:T(8,128)(2,1)S(1)}, u32[]{:S(2)}, u32[]{:S(2)}) %collective-permute-start) | collective-permute-done | bytes 262176 | tf_op jit(solution)/shard_map/ppermute | solution.py:15
  19.6 1.9 collective-permute-start.1
  21.6 10.5 %collective-permute-done.1 = bf16[2,256,256]{1,2,0:T(8,128)(2,1)S(1)} collective-permute-done((bf16[2,256,256]{1,2,0:T(8,128)(2,1)S(1)}, bf16[2,256,256]{1,2,0:T(8,128)(2,1)S(1)}, u32[]{:S(2)}, u32[]{:S(2)}) %collective-permute-start.1) | collective-permute-done | bytes 262176 | tf_op jit(solution)/shard_map/ppermute | solution.py:15
  32.0 1.9 collective-permute-start.2
  33.9 4.1 %copy.74 = bf16[256,4096]{0,1:T(8,128)(2,1)} copy(bf16[256,4096]{1,0:T(8,128)(2,1)} %param.7) | data formatting | bytes 4194304 | tf_op args[3]
  38.0 6.3 %all-to-all-start.1 = ((bf16[256,8,512]{0,2,1:T(8,128)(2,1)}), bf16[256,8,512]{0,2,1:T(8,128)(2,1)S(1)}, u32[]{:S(2)}, u32[]{:S(2)}) async-start(bf16[256,8,512]{0,2,1:T(8,128)(2,1)} %bitcast.67), calls=%async_computation.1 | async-start | bytes 4194304 | tf_op jit(solution)/shard_map/all_to_all | solution.py:73
  44.4 1.9 collective-permute-start.3
  46.4 55.1 %collective-permute-done.3 = bf16[2,256,256]{1,2,0:T(8,128)(2,1)S(1)} collective-permute-done((bf16[2,256,256]{1,2,0:T(8,128)(2,1)}, bf16[2,256,256]{1,2,0:T(8,128)(2,1)S(1)}, u32[]{:S(2)}, u32[]{:S(2)}) %collective-permute-start.3) | collective-permute-done | bytes 262176 | tf_op jit(solution)/shard_map/ppermute | solution.py:15
  101.5 1.9 collective-permute-start.4
  103.6 11.0 %collective-permute-done.4 = bf16[2,256,256]{1,2,0:T(8,128)(2,1)S(1)} collective-permute-done((bf16[2,256,256]{1,2,0:T(8,128)(2,1)S(1)}, bf16[2,256,256]{1,2,0:T(8,128)(2,1)S(1)}, u32[]{:S(2)}, u32[]{:S(2)}) %collective-permute-start.4) | collective-permute-done | bytes 262176 | tf_op jit(solution)/shard_map/ppermute | solution.py:15
  114.6 1.9 collective-permute-start.5
  116.6 10.3 %collective-permute-done.5 = bf16[2,256,256]{1,2,0:T(8,128)(2,1)} collective-permute-done((bf16[2,256,256]{1,2,0:T(8,128)(2,1)S(1)}, bf16[2,256,256]{1,2,0:T(8,128)(2,1)}, u32[]{:S(2)}, u32[]{:S(2)}) %collective-permute-start.5) | collective-permute-done | bytes 262176 | tf_op jit(solution)/shard_map/ppermute | solution.py:15
  126.9 1.9 collective-permute-start.6
  133.4 4.9 %collective-permute-done.6 = bf16[2,256,256]{1,2,0:T(8,128)(2,1)S(1)} collective-permute-done((bf16[2,256,256]{1,2,0:T(8,128)(2,1)}, bf16[2,256,256]{1,2,0:T(8,128)(2,1)S(1)}, u32[]{:S(2)}, u32[]{:S(2)}) %collective-permute-start.6) | collective-permute-done | bytes 262176 | tf_op jit(solution)/shard_map/ppermute | solution.py:15
  138.3 1.9 collective-permute-start.7
  141.2 1.1 pad_add_fusion
  142.3 7.4 %collective-permute-done.7 = bf16[2,256,256]{1,2,0:T(8,128)(2,1)S(1)} collective-permute-done((bf16[2,256,256]{1,2,0:T(8,128)(2,1)S(1)}, bf16[2,256,256]{1,2,0:T(8,128)(2,1)S(1)}, u32[]{:S(2)}, u32[]{:S(2)}) %collective-permute-start.7) | collective-permute-done | bytes 262176 | tf_op jit(solution)/shard_map/ppermute | solution.py:15
  149.7 1.0 constant_dynamic-update-slice_fusion.6
  150.7 1.0 constant_dynamic-update-slice_fusion.3
  151.8 1.2 fusion.53
  152.9 1.4 copy.67
  154.3 3.3 %exponential_reduce_fusion = f32[2,256]{1,0:T(2,128)S(1)} fusion(bf16[256,2,128]{0,2,1:T(8,128)(2,1)S(1)} %bitcast.85, pred[256,2560]{0,1:T(8,128)(4,1)} %pad_add_fusion, bf16[256,2,128]{2,0,1:T(8,128)(2,1)S(1)} %copy-done.12, bf16[2304,2,128]{2,0,1:T(8,128)(2,1)} %copy.67), kind=kOutput, calls=%fused_computation.7 | convolution fusion | flops 343411200 | bytes 2099200 | tf_op jit(solution)/shard_map/sub | solution.py:46
  157.6 4.9 %fusion.16 = bf16[2,128,256]{2,1,0:T(8,128)(2,1)} fusion(f32[2,256]{1,0:T(2,128)S(1)} %exponential_reduce_fusion, bf16[256,2,128]{0,2,1:T(8,128)(2,1)} %bitcast.86, bf16[2304,2,128]{0,2,1:T(8,128)(2,1)} %bitcast.75, bf16[256,2,128]{0,2,1:T(8,128)(2,1)} %bitcast.84, pred[256,2560]{0,1:T(8,128)(4,1)} %pad_add_fusion, bf16[256,2,128]{2,0,1:T(8,128)(2,1)S(1)} %copy-done.12, ...), kind=kOutput, calls=%fused_computation.23 | convolution fusion | flops 682953728 | bytes 3540992 | tf_op jit(solution)/shard_map/hqk,khd->qhd/dot_general | solution.py:48
  163.5 2.9 %fusion.58 = f32[2,256]{1,0:T(2,128)S(1)} fusion(bf16[2304,2,128]{0,2,1:T(8,128)(2,1)S(1)} %bitcast.70, bf16[256,2,128]{0,2,1:T(8,128)(2,1)S(1)} %bitcast.82, pred[256,2304]{0,1:T(8,128)(4,1)} %bitcast.78), kind=kOutput, calls=%fused_computation.66 | convolution fusion | flops 306710784 | bytes 1902592 | tf_op jit(solution)/shard_map/sub | solution.py:46
  166.4 4.4 %fusion.15 = bf16[2,128,256]{2,1,0:T(8,128)(2,1)} fusion(bf16[2304,2,128]{0,2,1:T(8,128)(2,1)} %bitcast.76, f32[2,256]{1,0:T(2,128)S(1)} %fusion.58, bf16[2304,2,128]{0,2,1:T(8,128)(2,1)S(1)} %bitcast.71, bf16[256,2,128]{0,2,1:T(8,128)(2,1)S(1)} %bitcast.83, pred[256,2304]{0,1:T(8,128)(4,1)} %bitcast.79), kind=kOutput, calls=%fused_computation.22 | convolution fusion | flops 609946368 | bytes 3213312 | tf_op jit(solution)/shard_map/hqk,khd->qhd/dot_general | solution.py:48
  171.9 1.5 stack.5
  173.5 5.2 %all-to-all-start = ((bf16[8,2,256,256]{3,2,1,0:T(8,128)(2,1)}), bf16[8,2,256,256]{3,2,1,0:T(8,128)(2,1)}, u32[]{:S(2)}, u32[]{:S(2)}) async-start(bf16[8,2,256,256]{3,2,1,0:T(8,128)(2,1)} %stack.5), calls=%async_computation | async-start | bytes 4194304 | tf_op jit(solution)/shard_map/all_to_all | solution.py:75
  178.7 2.4 %copy.75 = bf16[8,256,512]{2,1,0:T(8,128)(2,1)} copy(bf16[8,256,512]{1,2,0:T(8,128)(2,1)S(1)} %bitcast.66) | data formatting | bytes 4194304 | tf_op jit(solution)/shard_map/all_to_all | solution.py:73
  181.0 49.8 %all-to-all-done = bf16[8,2,256,256]{3,2,1,0:T(8,128)(2,1)} async-done(((bf16[8,2,256,256]{3,2,1,0:T(8,128)(2,1)}), bf16[8,2,256,256]{3,2,1,0:T(8,128)(2,1)}, u32[]{:S(2)}, u32[]{:S(2)}) %all-to-all-start) | async-done | bytes 2097184 | tf_op jit(solution)/shard_map/all_to_all | solution.py:75
  230.8 2.8 %copy.73 = bf16[2,256,8,256]{3,2,1,0:T(8,128)(2,1)S(1)} copy(bf16[2,256,8,256]{3,1,0,2:T(8,128)(2,1)} %bitcast.16) | data formatting | bytes 4194304 | tf_op jit(solution)/shard_map/reshape | solution.py:74
  235.2 2.0 convolution_convert_fusion
  (72 shorter events, 10.7 us)
Async XLA Ops:
  1.1 18.5 %collective-permute-start = (bf16[2,256,256]{1,2,0:T(8,128)(2,1)S(1)}, bf16[2,256,256]{1,2,0:T(8,128)(2,1)S(1)}, u32[]{:S(2)}, u32[]{:S(2)}) collective-permute-start(bf16[2,256,256]{1,2,0:T(8,128)(2,1)S(1)} %bitcast.77), channel_id=1, source_target_pairs={{0,8},{8,16},{16,24},{24,32},{32,40},{40,48},{48,56},{56,64},{64,7... | collective-permute-start | bytes 786440 | tf_op jit(solution)/shard_map/ppermute | solution.py:15
  19.6 18.4 %copy-start.3 = (bf16[2,256,256]{1,2,0:T(8,128)(2,1)}, bf16[2,256,256]{1,2,0:T(8,128)(2,1)S(1)}, u32[]{:S(2)}) copy-start(bf16[2,256,256]{1,2,0:T(8,128)(2,1)S(1)} %collective-permute-done) | copy-start | bytes 786436
  19.6 12.4 %collective-permute-start.1 = (bf16[2,256,256]{1,2,0:T(8,128)(2,1)S(1)}, bf16[2,256,256]{1,2,0:T(8,128)(2,1)S(1)}, u32[]{:S(2)}, u32[]{:S(2)}) collective-permute-start(bf16[2,256,256]{1,2,0:T(8,128)(2,1)S(1)} %collective-permute-done), channel_id=1, source_target_pairs={{0,8},{8,16},{16,24},{24,32},{32,40},{40,48},{48,56},{56,64},{64,7... | collective-permute-start | bytes 786440 | tf_op jit(solution)/shard_map/ppermute | solution.py:15
  32.0 6.0 %copy-start.5 = (bf16[2,256,256]{1,2,0:T(8,128)(2,1)}, bf16[2,256,256]{1,2,0:T(8,128)(2,1)S(1)}, u32[]{:S(2)}) copy-start(bf16[2,256,256]{1,2,0:T(8,128)(2,1)S(1)} %collective-permute-done.1) | copy-start | bytes 786436
  32.0 12.4 %collective-permute-start.2 = (bf16[2,256,256]{1,2,0:T(8,128)(2,1)S(1)}, bf16[2,256,256]{1,2,0:T(8,128)(2,1)}, u32[]{:S(2)}, u32[]{:S(2)}) collective-permute-start(bf16[2,256,256]{1,2,0:T(8,128)(2,1)S(1)} %collective-permute-done.1), channel_id=1, source_target_pairs={{0,8},{8,16},{16,24},{24,32},{32,40},{40,48},{48,56},{56,64},{64,7... | collective-permute-start | bytes 786440 | tf_op jit(solution)/shard_map/ppermute | solution.py:15
  38.0 65.4 %copy-start.15 = (s32[4,32]{1,0:T(4,128)S(1)}, s32[4,32]{1,0:T(4,128)}, u32[]{:S(2)}) copy-start(s32[4,32]{1,0:T(4,128)} %param.6) | copy-start | bytes 1540
  38.0 78.6 %copy-start.2 = (bf16[2,256,256]{2,1,0:T(8,128)(2,1)S(1)}, bf16[2,256,256]{2,1,0:T(8,128)(2,1)}, u32[]{:S(2)}) copy-start(bf16[2,256,256]{2,1,0:T(8,128)(2,1)} %param.4) | copy-start | bytes 786436
  38.0 93.0 %copy-start.1 = (bf16[2,2,256,256]{3,2,1,0:T(8,128)(2,1)S(1)}, bf16[2,2,256,256]{3,2,1,0:T(8,128)(2,1)}, u32[]{:S(2)}) copy-start(bf16[2,2,256,256]{3,2,1,0:T(8,128)(2,1)} %param.5) | copy-start | bytes 1572868
  38.0 133.9 %all-to-all-start.1 = ((bf16[256,8,512]{0,2,1:T(8,128)(2,1)}), bf16[256,8,512]{0,2,1:T(8,128)(2,1)S(1)}, u32[]{:S(2)}, u32[]{:S(2)}) async-start(bf16[256,8,512]{0,2,1:T(8,128)(2,1)} %bitcast.67), calls=%async_computation.1 | async-start | bytes 4194304 | tf_op jit(solution)/shard_map/all_to_all | solution.py:73
  44.4 57.1 %collective-permute-start.3 = (bf16[2,256,256]{1,2,0:T(8,128)(2,1)}, bf16[2,256,256]{1,2,0:T(8,128)(2,1)S(1)}, u32[]{:S(2)}, u32[]{:S(2)}) collective-permute-start(bf16[2,256,256]{1,2,0:T(8,128)(2,1)} %collective-permute-done.2), channel_id=1, source_target_pairs={{0,8},{8,16},{16,24},{24,32},{32,40},{40,48},{48,56},{56,64},{64,7... | collective-permute-start | bytes 786440 | tf_op jit(solution)/shard_map/ppermute | solution.py:15
  101.5 15.0 %copy-start.7 = (bf16[2,256,256]{1,2,0:T(8,128)(2,1)}, bf16[2,256,256]{1,2,0:T(8,128)(2,1)S(1)}, u32[]{:S(2)}) copy-start(bf16[2,256,256]{1,2,0:T(8,128)(2,1)S(1)} %collective-permute-done.3) | copy-start | bytes 786436
  101.5 13.0 %collective-permute-start.4 = (bf16[2,256,256]{1,2,0:T(8,128)(2,1)S(1)}, bf16[2,256,256]{1,2,0:T(8,128)(2,1)S(1)}, u32[]{:S(2)}, u32[]{:S(2)}) collective-permute-start(bf16[2,256,256]{1,2,0:T(8,128)(2,1)S(1)} %collective-permute-done.3), channel_id=1, source_target_pairs={{0,8},{8,16},{16,24},{24,32},{32,40},{40,48},{48,56},{56,64},{64,7... | collective-permute-start | bytes 786440 | tf_op jit(solution)/shard_map/ppermute | solution.py:15
  114.6 2.0 copy-start.9
  114.6 12.3 %collective-permute-start.5 = (bf16[2,256,256]{1,2,0:T(8,128)(2,1)S(1)}, bf16[2,256,256]{1,2,0:T(8,128)(2,1)}, u32[]{:S(2)}, u32[]{:S(2)}) collective-permute-start(bf16[2,256,256]{1,2,0:T(8,128)(2,1)S(1)} %collective-permute-done.4), channel_id=1, source_target_pairs={{0,8},{8,16},{16,24},{24,32},{32,40},{40,48},{48,56},{56,64},{64,7... | collective-permute-start | bytes 786440 | tf_op jit(solution)/shard_map/ppermute | solution.py:15
  126.9 11.5 %collective-permute-start.6 = (bf16[2,256,256]{1,2,0:T(8,128)(2,1)}, bf16[2,256,256]{1,2,0:T(8,128)(2,1)S(1)}, u32[]{:S(2)}, u32[]{:S(2)}) collective-permute-start(bf16[2,256,256]{1,2,0:T(8,128)(2,1)} %collective-permute-done.5), channel_id=1, source_target_pairs={{0,8},{8,16},{16,24},{24,32},{32,40},{40,48},{48,56},{56,64},{64,7... | collective-permute-start | bytes 786440 | tf_op jit(solution)/shard_map/ppermute | solution.py:15
  131.1 19.6 %copy-start.10 = (bf16[2,256,256]{1,2,0:T(8,128)(2,1)S(1)}, bf16[2,256,256]{1,2,0:T(8,128)(2,1)}, u32[]{:S(2)}) copy-start(bf16[2,256,256]{1,2,0:T(8,128)(2,1)} %copy-done.9) | copy-start | bytes 786436
  131.9 18.7 %copy-start.8 = (bf16[2,256,256]{1,2,0:T(8,128)(2,1)S(1)}, bf16[2,256,256]{1,2,0:T(8,128)(2,1)}, u32[]{:S(2)}) copy-start(bf16[2,256,256]{1,2,0:T(8,128)(2,1)} %copy-done.7) | copy-start | bytes 786436
  138.3 11.3 %collective-permute-start.7 = (bf16[2,256,256]{1,2,0:T(8,128)(2,1)S(1)}, bf16[2,256,256]{1,2,0:T(8,128)(2,1)S(1)}, u32[]{:S(2)}, u32[]{:S(2)}) collective-permute-start(bf16[2,256,256]{1,2,0:T(8,128)(2,1)S(1)} %collective-permute-done.6), channel_id=1, source_target_pairs={{0,8},{8,16},{16,24},{24,32},{32,40},{40,48},{48,56},{56,64},{64,7... | collective-permute-start | bytes 786440 | tf_op jit(solution)/shard_map/ppermute | solution.py:15
  141.1 10.6 %copy-start.6 = (bf16[2,256,256]{1,2,0:T(8,128)(2,1)S(1)}, bf16[2,256,256]{1,2,0:T(8,128)(2,1)}, u32[]{:S(2)}) copy-start(bf16[2,256,256]{1,2,0:T(8,128)(2,1)} %copy-done.5) | copy-start | bytes 786436
  141.2 10.6 %copy-start.4 = (bf16[2,256,256]{1,2,0:T(8,128)(2,1)S(1)}, bf16[2,256,256]{1,2,0:T(8,128)(2,1)}, u32[]{:S(2)}) copy-start(bf16[2,256,256]{1,2,0:T(8,128)(2,1)} %copy-done.3) | copy-start | bytes 786436
  152.9 1.4 copy-start.12
  152.9 1.4 copy-start.13
  157.6 5.9 %copy-start.11 = (bf16[1,256,256]{1,2,0:T(8,128)(2,1)S(1)}, bf16[1,256,256]{1,2,0:T(8,128)(2,1)}, u32[]{:S(2)}) copy-start(bf16[1,256,256]{1,2,0:T(8,128)(2,1)} %copy.82) | copy-start | bytes 393220
  166.4 4.4 %copy-start.14 = (bf16[2,128,256]{2,1,0:T(8,128)(2,1)S(1)}, bf16[2,128,256]{2,1,0:T(8,128)(2,1)}, u32[]{:S(2)}) copy-start(bf16[2,128,256]{2,1,0:T(8,128)(2,1)} %fusion.16) | copy-start | bytes 393220
  173.5 57.4 %all-to-all-start = ((bf16[8,2,256,256]{3,2,1,0:T(8,128)(2,1)}), bf16[8,2,256,256]{3,2,1,0:T(8,128)(2,1)}, u32[]{:S(2)}, u32[]{:S(2)}) async-start(bf16[8,2,256,256]{3,2,1,0:T(8,128)(2,1)} %stack.5), calls=%async_computation | async-start | bytes 4194304 | tf_op jit(solution)/shard_map/all_to_all | solution.py:75
  233.6 1.6 copy-start
